TPU v7x, 32 devices: a whole 2x2x4 slice. The times are simulated.
32 devices in a mesh: mem: 8 (over z, x), head: 4 (over y, core).
Axes of the slice: x: 2, y: 2, z: 4, core: 2. Of those that a mesh axis runs over, the one named last changes fastest.
Arguments:
- tokens: bfloat16 [8192, 4096], P('mem'), may hold values from -14 to 14
- w_query: bfloat16 [4096, 4096], P(None, 'head'), may hold values from -0.09375 to 0.09375
- w_key: bfloat16 [4096, 1024], P(None, 'head'), may hold values from -0.09375 to 0.09375
- w_value: bfloat16 [4096, 1024], P(None, 'head'), may hold values from -0.09375 to 0.09375
- w_out: bfloat16 [4096, 4096], P('head'), may hold values from -0.09375 to 0.09375
- gate_bias: float32 [32], P('head'), may hold values from -4 to 4
- mem_keys: bfloat16 [65536, 1024], P('mem', 'head'), may hold values from -72 to 72
- mem_values: bfloat16 [65536, 1024], P('mem', 'head'), may hold values from -6 to 6
- block_ids: int32 [64, 16], P('mem'), may hold values from 0 to 511, as said below
- block_counts: int32 [512], replicated, may hold values from 1 to 128
Outputs:
- layer_out: bfloat16 [8192, 4096], P('mem', 'head')
Inputs may be any that keep to these rules, and one draw needn't show every extreme that they name: `block_ids`: row c lists 16 different memory blocks; block b lies on index b // 64 of mem. Over the 8 query blocks of one index of mem, every listed block appears in exactly two rows, at most 16 different listed blocks lie on any one index of mem, and in every draw some index of mem has exactly 16 different blocks listed by every index of mem.
All inputs are finite; a program needn't handle non-finite values.
Results may differ from a plain program's by a relative error of at most 0.015.
The roundings to bfloat16 on the way count: a program that leaves them out, or rounds other values in their place, can miss the bound.
Values may be sent and summed in bfloat16 or wider, within the bound.
A program may use at most 320 MiB of HBM per device.

v0:
```python
import jax
import jax.numpy as jnp
from jax import lax
from jax.sharding import PartitionSpec as P

HD = 128
BLK = 128


def attend(queries, key_rows, value_rows, allowed):
    scores = jnp.einsum(
        "qkgd,skd->kgqs", queries, key_rows, preferred_element_type=jnp.float32
    ) * HD ** (-0.5)
    scores = jnp.where(allowed, scores, -jnp.inf)
    peak_score = jnp.max(scores, axis=-1, keepdims=True)
    weights = jnp.exp(scores - peak_score)
    weights = (weights / jnp.sum(weights, axis=-1, keepdims=True)).astype(jnp.bfloat16)
    return jnp.einsum("kgqs,skd->qkgd", weights, value_rows, preferred_element_type=jnp.float32)


def plan_requests(flat_chosen, blocks_each):
    owner_of = flat_chosen // blocks_each
    local_of = flat_chosen % blocks_each
    order = jnp.arange(flat_chosen.shape[0])
    earlier = order[None, :] < order[:, None]
    first_seen = jnp.ones(flat_chosen.shape, jnp.bool_)
    same_owner = owner_of[:, None] == owner_of[None, :]
    first_rank = jnp.sum((same_owner & earlier & first_seen[None, :]).astype(jnp.int32), axis=1)
    return (owner_of, local_of, first_rank, first_seen)


def on_device(
    tokens, w_query, w_key, w_value, w_out, gate_bias, mem_keys, mem_values, block_ids, block_counts
):
    tok_rows = tokens.shape[0]
    qblk_count = tok_rows // BLK
    topk_count = block_ids.shape[1]
    kv_local = w_key.shape[1] // HD
    heads_local = w_query.shape[1] // HD
    per_kv = heads_local // kv_local
    owners = lax.axis_size("mem")
    blocks_each = mem_keys.shape[0] // BLK
    me_index = lax.axis_index("mem")
    block_cap = max(2, topk_count * qblk_count // owners)
    capacity = 2 * block_cap
    all_chosen = lax.all_gather(block_ids, "mem", axis=0, tiled=True).reshape(
        owners, qblk_count * topk_count
    )

    def send_list(flat_chosen):
        owner_of, local_of, rank_of, first_seen = plan_requests(flat_chosen, blocks_each)
        wanted = (owner_of == me_index) & first_seen
        select = wanted[None, :] & (rank_of[None, :] == jnp.arange(capacity)[:, None])
        return jnp.sum(select.astype(jnp.int32) * local_of[None, :], axis=1)

    send_slots = jax.vmap(send_list)(all_chosen)
    key_blocks = mem_keys.reshape(blocks_each, BLK, kv_local * HD)
    value_blocks = mem_values.reshape(blocks_each, BLK, kv_local * HD)
    send_keys = key_blocks[send_slots]
    send_values = value_blocks[send_slots]
    got_keys, got_values = (
        lax.all_to_all(send_keys, "mem", split_axis=0, concat_axis=0, tiled=True),
        lax.all_to_all(send_values, "mem", split_axis=0, concat_axis=0, tiled=True),
    )
    queries = jnp.dot(tokens, w_query, preferred_element_type=jnp.float32).astype(jnp.bfloat16)
    local_keys = jnp.dot(tokens, w_key, preferred_element_type=jnp.float32).astype(jnp.bfloat16)
    local_values = jnp.dot(tokens, w_value, preferred_element_type=jnp.float32).astype(jnp.bfloat16)
    causal = jnp.arange(tok_rows)[None, :] <= jnp.arange(tok_rows)[:, None]
    local_out = attend(
        queries.reshape(tok_rows, kv_local, per_kv, HD),
        local_keys.reshape(tok_rows, kv_local, HD),
        local_values.reshape(tok_rows, kv_local, HD),
        causal[None, None],
    )
    own_flat = block_ids.reshape(-1)
    owner_of, local_of, rank_of, first_seen = plan_requests(own_flat, blocks_each)
    slot_of = owner_of * capacity + rank_of
    key_rows = got_keys.reshape(owners * capacity, BLK, kv_local * HD)[slot_of]
    value_rows = got_values.reshape(owners * capacity, BLK, kv_local * HD)[slot_of]
    key_rows = key_rows.reshape(qblk_count, topk_count * BLK, kv_local, HD)
    value_rows = value_rows.reshape(qblk_count, topk_count * BLK, kv_local, HD)
    total_blocks = block_counts.shape[0]
    filled = jnp.sum(
        jnp.where(own_flat[:, None] == jnp.arange(total_blocks)[None, :], block_counts[None, :], 0),
        axis=1,
    )
    allowed_mem = (jnp.arange(BLK)[None, :] < filled[:, None]).reshape(qblk_count, topk_count * BLK)

    def memory_block(inputs):
        q_blk, k_blk, v_blk, allow_blk = inputs
        return attend(q_blk, k_blk, v_blk, allow_blk[None, None, None, :])

    mem_out = lax.map(
        memory_block,
        (queries.reshape(qblk_count, BLK, kv_local, per_kv, HD), key_rows, value_rows, allowed_mem),
    )
    mem_out = mem_out.reshape(tok_rows, kv_local, per_kv, HD)
    gate = jax.nn.sigmoid(gate_bias).reshape(kv_local, per_kv)[None, :, :, None]
    attn = (
        (gate * mem_out + (1.0 - gate) * local_out)
        .astype(jnp.bfloat16)
        .reshape(tok_rows, heads_local * HD)
    )
    terms = jnp.dot(attn, w_out, preferred_element_type=jnp.float32)
    return lax.psum_scatter(terms.astype(jnp.bfloat16), "head", scatter_dimension=1, tiled=True)


def solution(mesh):
    in_specs = (
        P("mem", None),
        P(None, "head"),
        P(None, "head"),
        P(None, "head"),
        P("head", None),
        P("head"),
        P("mem", "head"),
        P("mem", "head"),
        P("mem", None),
        P(),
    )
    out_specs = P("mem", "head")
    return jax.shard_map(
        on_device, mesh=mesh, in_specs=in_specs, out_specs=out_specs, check_vma=False
    )
```

profile of v0, /device:TPU:0, one launch (start us, length us, event | category | flops | bytes accessed | tf_op | source)
XLA Modules:
  0.0 1164.7 jit_solution(14783743435537035418)
XLA Ops:
  6.6 32.5 %all_gather.3 = s32[64,16]{1,0:T(8,128)S(1)} all-gather(s32[8,16]{1,0:T(8,128)} %param.20), channel_id=1, replica_groups=mesh['mem'=8,'head'=4] {'mem'}, dimensions={0}, use_global_device_ids=true | all-gather | bytes 4608 | tf_op jit(solution)/shard_map/all_gather | solution.py:46
  39.8 11.5 gather_fusion
  51.3 5.7 all-to-all-start
  57.0 11.6 gather_fusion.2
  68.6 345.2 %all-to-all-done = bf16[8,32,128,256]{3,2,1,0:T(8,128)(2,1)} async-done(((bf16[8,32,128,256]{3,2,1,0:T(8,128)(2,1)}), bf16[8,32,128,256]{3,2,1,0:T(8,128)(2,1)}, u32[]{:S(2)}, u32[]{:S(2)}) %all-to-all-start) | async-done | bytes 16777248 | tf_op jit(solution)/shard_map/all_to_all | solution.py:63
  413.8 5.9 all-to-all-start.1
  420.1 13.8 %convolution_convert_fusion.1 = bf16[1024,1024]{0,1:T(8,128)(2,1)S(1)} fusion(bf16[1024,4096]{1,0:T(8,128)(2,1)} %param.12, bf16[4096,1024]{1,0:T(8,128)(2,1)} %param.13), kind=kOutput, calls=%fused_computation.40 | convolution fusion | flops 8590983168 | bytes 18874368 | tf_op jit(solution)/shard_map/dot_general | solution.py:65
  437.2 4.3 copy.44
  443.2 6.7 convolution_convert_fusion.2
  449.9 6.7 convolution_convert_fusion.3
  456.7 19.2 %fusion.32 = (f32[2,4,1024]{2,1,0:T(4,128)S(1)}, f32[2,4,1024,1024]{2,3,1,0:T(8,128)}) fusion(pred[1024,1024]{0,1:T(8,128)(4,1)S(1)} %iota_compare_fusion, bf16[1024,2,128,1]{0,2,3,1:T(8,128)(2,1)} %bitcast.120, bf16[1024,2,4,128]{0,3,2,1:T(8,128)(2,1)S(1)} %bitcast.117), kind=kOutput, calls=%fused_computation.81 | convolution fusion | flops 2181039104 | bytes 37257216 | tf_op jit(solution)/shard_map/sub | solution.py:16
  475.9 12.3 %gather_fusion.1 = bf16[128,128,256]{2,1,0:T(8,128)(2,1)} fusion(bf16[256,128,256]{2,1,0:T(8,128)(2,1)} %bitcast.13, s32[1024]{0:T(1024)S(1)} %pad_clamp_fusion), kind=kCustom, calls=%fused_computation.1 | custom fusion | bytes 16777728 | tf_op jit(solution)/shard_map/gather | solution.py:79
  488.2 12.5 %reshape.370 = bf16[8,2048,2,128]{3,2,1,0:T(2,128)(2,1)} reshape(bf16[128,128,256]{2,1,0:T(8,128)(2,1)} %gather_fusion.1) | data formatting | bytes 16777216 | tf_op jit(solution)/shard_map/reshape | solution.py:81
  500.7 279.9 %all-to-all-done.1 = bf16[8,32,128,256]{3,2,1,0:T(8,128)(2,1)} async-done(((bf16[8,32,128,256]{3,2,1,0:T(8,128)(2,1)}), bf16[8,32,128,256]{3,2,1,0:T(8,128)(2,1)}, u32[]{:S(2)}, u32[]{:S(2)}) %all-to-all-start.1) | async-done | bytes 16777248 | tf_op jit(solution)/shard_map/all_to_all | solution.py:62
  780.6 12.3 %gather_fusion.3 = bf16[128,128,256]{2,1,0:T(8,128)(2,1)} fusion(bf16[256,128,256]{2,1,0:T(8,128)(2,1)} %bitcast.20, s32[1024]{0:T(1024)S(1)} %pad_clamp_fusion), kind=kCustom, calls=%fused_computation.3 | custom fusion | bytes 16777728 | tf_op jit(solution)/shard_map/gather | solution.py:78
  793.0 12.5 %reshape.371 = bf16[8,2048,2,128]{3,2,1,0:T(2,128)(2,1)} reshape(bf16[128,128,256]{2,1,0:T(8,128)(2,1)} %gather_fusion.3) | data formatting | bytes 16777216 | tf_op jit(solution)/shard_map/reshape | solution.py:80
  805.5 246.9 %while.10 = (s32[]{:T(128)}, f32[8,128,2,4,128]{1,0,4,3,2:T(8,128)}, bf16[8,2048,2,128]{3,2,1,0:T(2,128)(2,1)}, pred[8,2048]{1,0:T(8,128)(4,1)S(1)}, bf16[8,2048...) while((s32[]{:T(128)}, f32[8,128,2,4,128]{1,0,4,3,2:T(8,128)}, ...), condition=%wide.region_7.8_spmd, body=%wide.region_4.7_spmd.sunk | while | flops 1090521088 | bytes 43792992 | solution.py:93
  805.6 2.7 constant_dynamic-slice_fusion.3
  810.6 5.9 fusion.54
  817.3 4.1 fusion.55
  821.4 15.1 %dynamic_update_slice.5 = f32[8,128,2,4,128]{1,0,4,3,2:T(8,128)} dynamic-update-slice(f32[8,128,2,4,128]{1,0,4,3,2:T(8,128)} %get-tuple-element.136, f32[1,128,2,4,128]{1,0,4,3,2:T(1,128)S(1)} %bitcast.114, s32[]{:T(128)} %get-tuple-element.135, s32[]{:T(128)} %constant.69.clone.1..sunk, s32[]{:T(128)} %constant.69.clone.1..sunk, s32[]{:T(128)} %constant.69.clone.1..sunk, s32[]{:T(128)} %constant.69.clone.1..sunk) | dynamic-update-slice | bytes 1048580 | tf_op jit(solution)/shard_map/while/body/jit(dynamic_update_index_in_dim)/dynamic_update_slice | solution.py:93
  836.5 2.7 constant_dynamic-slice_fusion.3
  841.4 5.9 fusion.54
  848.1 4.1 fusion.55
  852.2 15.1 %dynamic_update_slice.5 = f32[8,128,2,4,128]{1,0,4,3,2:T(8,128)} dynamic-update-slice(f32[8,128,2,4,128]{1,0,4,3,2:T(8,128)} %get-tuple-element.136, f32[1,128,2,4,128]{1,0,4,3,2:T(1,128)S(1)} %bitcast.114, s32[]{:T(128)} %get-tuple-element.135, s32[]{:T(128)} %constant.69.clone.1..sunk, s32[]{:T(128)} %constant.69.clone.1..sunk, s32[]{:T(128)} %constant.69.clone.1..sunk, s32[]{:T(128)} %constant.69.clone.1..sunk) | dynamic-update-slice | bytes 1048580 | tf_op jit(solution)/shard_map/while/body/jit(dynamic_update_index_in_dim)/dynamic_update_slice | solution.py:93
  872.3 5.9 fusion.54
  879.0 4.1 fusion.55
  883.1 15.1 %dynamic_update_slice.5 = f32[8,128,2,4,128]{1,0,4,3,2:T(8,128)} dynamic-update-slice(f32[8,128,2,4,128]{1,0,4,3,2:T(8,128)} %get-tuple-element.136, f32[1,128,2,4,128]{1,0,4,3,2:T(1,128)S(1)} %bitcast.114, s32[]{:T(128)} %get-tuple-element.135, s32[]{:T(128)} %constant.69.clone.1..sunk, s32[]{:T(128)} %constant.69.clone.1..sunk, s32[]{:T(128)} %constant.69.clone.1..sunk, s32[]{:T(128)} %constant.69.clone.1..sunk) | dynamic-update-slice | bytes 1048580 | tf_op jit(solution)/shard_map/while/body/jit(dynamic_update_index_in_dim)/dynamic_update_slice | solution.py:93
  903.1 5.9 fusion.54
  909.8 4.1 fusion.55
  913.9 15.1 %dynamic_update_slice.5 = f32[8,128,2,4,128]{1,0,4,3,2:T(8,128)} dynamic-update-slice(f32[8,128,2,4,128]{1,0,4,3,2:T(8,128)} %get-tuple-element.136, f32[1,128,2,4,128]{1,0,4,3,2:T(1,128)S(1)} %bitcast.114, s32[]{:T(128)} %get-tuple-element.135, s32[]{:T(128)} %constant.69.clone.1..sunk, s32[]{:T(128)} %constant.69.clone.1..sunk, s32[]{:T(128)} %constant.69.clone.1..sunk, s32[]{:T(128)} %constant.69.clone.1..sunk) | dynamic-update-slice | bytes 1048580 | tf_op jit(solution)/shard_map/while/body/jit(dynamic_update_index_in_dim)/dynamic_update_slice | solution.py:93
  929.0 2.7 constant_dynamic-slice_fusion.3
  934.0 5.9 fusion.54
  940.7 4.1 fusion.55
  944.8 15.1 %dynamic_update_slice.5 = f32[8,128,2,4,128]{1,0,4,3,2:T(8,128)} dynamic-update-slice(f32[8,128,2,4,128]{1,0,4,3,2:T(8,128)} %get-tuple-element.136, f32[1,128,2,4,128]{1,0,4,3,2:T(1,128)S(1)} %bitcast.114, s32[]{:T(128)} %get-tuple-element.135, s32[]{:T(128)} %constant.69.clone.1..sunk, s32[]{:T(128)} %constant.69.clone.1..sunk, s32[]{:T(128)} %constant.69.clone.1..sunk, s32[]{:T(128)} %constant.69.clone.1..sunk) | dynamic-update-slice | bytes 1048580 | tf_op jit(solution)/shard_map/while/body/jit(dynamic_update_index_in_dim)/dynamic_update_slice | solution.py:93
  964.8 5.9 fusion.54
  971.5 4.1 fusion.55
  975.6 15.1 %dynamic_update_slice.5 = f32[8,128,2,4,128]{1,0,4,3,2:T(8,128)} dynamic-update-slice(f32[8,128,2,4,128]{1,0,4,3,2:T(8,128)} %get-tuple-element.136, f32[1,128,2,4,128]{1,0,4,3,2:T(1,128)S(1)} %bitcast.114, s32[]{:T(128)} %get-tuple-element.135, s32[]{:T(128)} %constant.69.clone.1..sunk, s32[]{:T(128)} %constant.69.clone.1..sunk, s32[]{:T(128)} %constant.69.clone.1..sunk, s32[]{:T(128)} %constant.69.clone.1..sunk) | dynamic-update-slice | bytes 1048580 | tf_op jit(solution)/shard_map/while/body/jit(dynamic_update_index_in_dim)/dynamic_update_slice | solution.py:93
  995.7 5.9 fusion.54
  1002.3 4.1 fusion.55
  1006.5 15.1 %dynamic_update_slice.5 = f32[8,128,2,4,128]{1,0,4,3,2:T(8,128)} dynamic-update-slice(f32[8,128,2,4,128]{1,0,4,3,2:T(8,128)} %get-tuple-element.136, f32[1,128,2,4,128]{1,0,4,3,2:T(1,128)S(1)} %bitcast.114, s32[]{:T(128)} %get-tuple-element.135, s32[]{:T(128)} %constant.69.clone.1..sunk, s32[]{:T(128)} %constant.69.clone.1..sunk, s32[]{:T(128)} %constant.69.clone.1..sunk, s32[]{:T(128)} %constant.69.clone.1..sunk) | dynamic-update-slice | bytes 1048580 | tf_op jit(solution)/shard_map/while/body/jit(dynamic_update_index_in_dim)/dynamic_update_slice | solution.py:93
  1026.5 5.9 fusion.54
  1033.2 4.1 fusion.55
  1037.3 15.1 %dynamic_update_slice.5 = f32[8,128,2,4,128]{1,0,4,3,2:T(8,128)} dynamic-update-slice(f32[8,128,2,4,128]{1,0,4,3,2:T(8,128)} %get-tuple-element.136, f32[1,128,2,4,128]{1,0,4,3,2:T(1,128)S(1)} %bitcast.114, s32[]{:T(128)} %get-tuple-element.135, s32[]{:T(128)} %constant.69.clone.1..sunk, s32[]{:T(128)} %constant.69.clone.1..sunk, s32[]{:T(128)} %constant.69.clone.1..sunk, s32[]{:T(128)} %constant.69.clone.1..sunk) | dynamic-update-slice | bytes 1048580 | tf_op jit(solution)/shard_map/while/body/jit(dynamic_update_index_in_dim)/dynamic_update_slice | solution.py:93
  1052.4 5.0 reshape.327
  1057.4 13.3 %fusion.22 = bf16[1024,2,4,128]{0,3,2,1:T(8,128)(2,1)S(1)} fusion(f32[1024,2,4,128]{0,3,2,1:T(8,128)} %reshape.327, bf16[1024,2,128,1]{0,2,3,1:T(8,128)(2,1)S(1)} %bitcast.119, f32[2,4,1024,1024]{2,3,1,0:T(8,128)} %get-tuple-element.81, f32[2,4,1024]{2,1,0:T(4,128)S(1)} %get-tuple-element.80, f32[2,4]{1,0:T(2,128)S(1)} %copy-done.8, f32[2,4]{1,0:T(2,128)S(1)} %copy-done.7), kind=kOutput, calls=%fused_computation.37 | convolution fusion | flops 2168455168 | bytes 40403008 | tf_op jit(solution)/shard_map/kgqs,skd->qkgd/dot_general | solution.py:18
  1070.7 14.9 %convolution_convert_fusion = bf16[1024,4096]{1,0:T(8,128)(2,1)} fusion(bf16[1024,1024]{0,1:T(8,128)(2,1)S(1)} %bitcast.118, bf16[1024,4096]{1,0:T(8,128)(2,1)} %param.16), kind=kOutput, calls=%fused_computation.35 | convolution fusion | flops 8594128896 | bytes 18874368 | tf_op jit(solution)/shard_map/dot_general | solution.py:104
  1085.7 71.9 %reduce-scatter.2.cloned.1.call-done = bf16[1024,1024]{1,0:T(8,128)(2,1)} async-done(((bf16[1024,4096]{1,0:T(8,128)(2,1)}), bf16[1024,1024]{1,0:T(8,128)(2,1)}) %reduce-scatter.2.cloned.1.call-update) | async-done | bytes 2097168 | tf_op jit(solution)/shard_map/reduce_scatter | solution.py:105
  (81 shorter events, 44.0 us)
Async XLA Ops:
  6.5 436.7 %copy-start = (bf16[4096,256]{1,0:T(8,128)(2,1)S(1)}, bf16[4096,256]{1,0:T(8,128)(2,1)}, u32[]{:S(2)}) copy-start(bf16[4096,256]{1,0:T(8,128)(2,1)} %param.14) | copy-start | bytes 6291460
  51.3 362.5 %all-to-all-start = ((bf16[8,32,128,256]{3,2,1,0:T(8,128)(2,1)}), bf16[8,32,128,256]{3,2,1,0:T(8,128)(2,1)}, u32[]{:S(2)}, u32[]{:S(2)}) async-start(bf16[8,32,128,256]{3,2,1,0:T(8,128)(2,1)} %bitcast.111), calls=%async_computation | async-start | bytes 33554432 | tf_op jit(solution)/shard_map/all_to_all | solution.py:63
  413.8 6.2 copy-start.4
  413.8 366.9 %all-to-all-start.1 = ((bf16[8,32,128,256]{3,2,1,0:T(8,128)(2,1)}), bf16[8,32,128,256]{3,2,1,0:T(8,128)(2,1)}, u32[]{:S(2)}, u32[]{:S(2)}) async-start(bf16[8,32,128,256]{3,2,1,0:T(8,128)(2,1)} %bitcast.110), calls=%async_computation.1 | async-start | bytes 33554432 | tf_op jit(solution)/shard_map/all_to_all | solution.py:62
  419.6 738.0 %reduce-scatter.2.cloned.1.call-start = ((), (), s32[]{:S(2)}) async-start(), calls=%async_computation.3 | async-start | bytes 10485760 | tf_op jit(solution)/shard_map/reduce_scatter | solution.py:105
  433.9 1.3 copy-start.2
  433.9 7.6 copy-start.5
  433.9 7.9 copy-start.10
  441.9 0.6 copy-start.6
  443.2 6.7 copy-start.9
  449.9 6.7 copy-start.3
  1052.4 5.0 copy-start.7
  1052.4 5.0 copy-start.8
  1052.4 5.0 copy-start.11
  1070.7 86.9 %copy-start.1 = (bf16[4096,256]{1,0:T(8,128)(2,1)S(1)}, bf16[4096,256]{1,0:T(8,128)(2,1)}, u32[]{:S(2)}) copy-start(bf16[4096,256]{1,0:T(8,128)(2,1)} %param.14) | copy-start | bytes 6291460
Sparse Core Ops, SparseCore 0:
  1085.8 71.7 reduce-scatter.1
where the time goes:
time: 1170 us; the launch traced here: 1160 us
  waiting for transfers between devices  697 us (60%)
  local copies, waits for them, and re-layouts  235 us (20%)
  matrix products  125 us (11%)
  other arithmetic  48.9 us (4%)
  blocking collectives  32.5 us (3%)
  between operations  13.8 us (1%)
  starting transfers between devices  11.9 us (1%)
    all_to_all x1, waiting for transfers between devices, on_device(): lax.all_to_all(send_values, 'mem', split_axis=0, concat_axis=0, tiled=True)  345 us
    all_to_all x1, waiting for transfers between devices, on_device(): lax.all_to_all(send_keys, 'mem', split_axis=0, concat_axis=0, tiled=True)  280 us
    dynamic_update_slice x8, local copies, waits for them, and re-layouts, on_device(): lax.map(memory_block, (queries.reshape(qblk_count, BLK, kv_local, per_kv,...  121 us
    reduce_scatter x1, waiting for transfers between devices, on_device(): lax.psum_scatter(terms.astype(jnp.bfloat16), 'head', scatter_dimension=1,...  71.9 us
    sub x8, other arithmetic, attend(): weights = jnp.exp(scores - peak_score)  46.9 us
    dot_general x9, matrix products, attend(): jnp.einsum('kgqs,skd->qkgd', weights, value_rows, preferred_element_type=...  46.1 us
    all_gather x1, blocking collectives, on_device(): lax.all_gather(block_ids, 'mem', axis=0, tiled=True)  32.5 us
    dynamic_slice x24, local copies, waits for them, and re-layouts, on_device(): lax.map(memory_block, (queries.reshape(qblk_count, BLK, kv_local, per_kv,...  28.1 us
  transfers between devices with their start and end apart: 3, of which 3 were waited for; matrix products, arithmetic and copies ran while one was open for 8% of the time, Pallas kernels for 0%

commit v1 on v0

--- a/solution.py
+++ b/solution.py
@@ -1,3 +1,4 @@
+import functools
 import jax
 import jax.numpy as jnp
 from jax import lax
@@ -5,6 +6,29 @@
 
 HD = 128
 BLK = 128
+
+
+def choose_windows(local_x, axis_key, dimension_no, pos_dim):
+    out_arr, d_next = (lax.axis_size(axis_key), lax.axis_index(axis_key))
+    tall = local_x.shape[dimension_no] // out_arr
+    top = list(local_x.shape)
+    top[dimension_no] = tall
+    raw_out = top[pos_dim]
+    top[pos_dim] = raw_out * out_arr
+    e_next = jnp.zeros(top, local_x.dtype)
+    for k in range(out_arr):
+        newest = lax.dynamic_slice_in_dim(local_x, (d_next ^ k) * tall, tall, axis=dimension_no)
+        if k:
+            block_now = map(lambda i0: (i0, i0 ^ k), range(out_arr))
+            o_now = list(block_now)
+            newest = lax.ppermute(newest, axis_key, o_now)
+        e_next = lax.dynamic_update_slice_in_dim(
+            e_next, newest, (d_next ^ k) * raw_out, axis=pos_dim
+        )
+    return e_next
+
+
+turn_terms = functools.partial(choose_windows, axis_key="mem", dimension_no=0, pos_dim=0)
 
 
 def attend(queries, key_rows, value_rows, allowed):
@@ -60,7 +84,7 @@
     send_values = value_blocks[send_slots]
     got_keys, got_values = (
         lax.all_to_all(send_keys, "mem", split_axis=0, concat_axis=0, tiled=True),
-        lax.all_to_all(send_values, "mem", split_axis=0, concat_axis=0, tiled=True),
+        turn_terms(send_values),
     )
     queries = jnp.dot(tokens, w_query, preferred_element_type=jnp.float32).astype(jnp.bfloat16)
     local_keys = jnp.dot(tokens, w_key, preferred_element_type=jnp.float32).astype(jnp.bfloat16)

time: 1170 us -> 1190 us (1.017)
  local copies, waits for them, and re-layouts: 235 us -> 270 us
  waiting for transfers between devices: 697 us -> 670 us
  starting transfers between devices: 11.9 us -> 26.2 us
    ppermute x0 -> x7, waiting for transfers between devices: none -> 518 us  [choose_windows(): newest = lax.ppermute(newest, axis_key, o_now)]
    all_to_all x1 -> x0, waiting for transfers between devices: 345 us -> none  [on_device(): lax.all_to_all(send_values, 'mem', split_axis=0, concat_axis=0, tiled=True)]
    all_to_all x1, waiting for transfers between devices: 280 us -> 0.01 us  [on_device(): lax.all_to_all(send_keys, 'mem', split_axis=0, concat_axis=0, tiled=True)]
    reduce_scatter x1, waiting for transfers between devices: 71.9 us -> 152 us  [on_device(): lax.psum_scatter(terms.astype(jnp.bfloat16), 'head', scatter_dimension=1,...]
    dynamic_update_slice x0 -> x7, local copies, waits for them, and re-layouts: none -> 20.5 us  [choose_windows(): lax.dynamic_update_slice_in_dim(e_next, newest, (d_next ^ k) * raw_out, a...]
    ppermute x0 -> x7, starting transfers between devices: none -> 20.2 us  [choose_windows(): newest = lax.ppermute(newest, axis_key, o_now)]
  transfers between devices with their start and end apart: 3 -> 9, of which waited for: 3 -> 6; matrix products, arithmetic and copies ran while one was open for 8% -> 10% of each run, Pallas kernels for 0% -> 0%
where the time goes in v1:
time: 1190 us
  waiting for transfers between devices  670 us (56%)
  local copies, waits for them, and re-layouts  270 us (23%)
  matrix products  125 us (11%)
  other arithmetic  48.9 us (4%)
  blocking collectives  32.5 us (3%)
  starting transfers between devices  26.2 us (2%)
  between operations  13.8 us (1%)
    ppermute x7, waiting for transfers between devices, choose_windows(): newest = lax.ppermute(newest, axis_key, o_now)  518 us
    reduce_scatter x1, waiting for transfers between devices, on_device(): lax.psum_scatter(terms.astype(jnp.bfloat16), 'head', scatter_dimension=1,...  152 us
    dynamic_update_slice x8, local copies, waits for them, and re-layouts, on_device(): lax.map(memory_block, (queries.reshape(qblk_count, BLK, kv_local, per_kv,...  121 us
    sub x8, other arithmetic, attend(): weights = jnp.exp(scores - peak_score)  46.9 us
    dot_general x9, matrix products, attend(): jnp.einsum('kgqs,skd->qkgd', weights, value_rows, preferred_element_type=...  46.1 us
    all_gather x1, blocking collectives, on_device(): lax.all_gather(block_ids, 'mem', axis=0, tiled=True)  32.5 us
    dynamic_slice x24, local copies, waits for them, and re-layouts, on_device(): lax.map(memory_block, (queries.reshape(qblk_count, BLK, kv_local, per_kv,...  28.1 us
  transfers between devices with their start and end apart: 9, of which 6 were waited for; matrix products, arithmetic and copies ran while one was open for 10% of the time, Pallas kernels for 0%

profile of v1, /device:TPU:0, one launch (start us, length us, event | category | flops | bytes accessed | tf_op | source)
XLA Modules:
  0.0 1186.6 jit_solution(16049246838863786012)
XLA Ops:
  6.6 32.5 %all_gather.3 = s32[64,16]{1,0:T(8,128)S(1)} all-gather(s32[8,16]{1,0:T(8,128)} %param.20), channel_id=1, replica_groups=mesh['mem'=8,'head'=4] {'mem'}, dimensions={0}, use_global_device_ids=true | all-gather | bytes 4608 | tf_op jit(solution)/shard_map/all_gather | solution.py:70
  39.8 11.6 gather_fusion.2
  51.4 5.7 all-to-all-start
  57.5 11.5 gather_fusion
  68.9 8.4 broadcast_in_dim.42
  80.4 6.0 constant_dynamic-slice_fusion.2
  95.5 6.6 convolution_convert_fusion.2
  102.1 13.8 %convolution_convert_fusion.1 = bf16[1024,1024]{0,1:T(8,128)(2,1)S(1)} fusion(bf16[1024,4096]{1,0:T(8,128)(2,1)} %param.12, bf16[4096,1024]{1,0:T(8,128)(2,1)} %param.13), kind=kOutput, calls=%fused_computation.41 | convolution fusion | flops 8590983168 | bytes 18874368 | tf_op jit(solution)/shard_map/dot_general | solution.py:89
  115.8 19.4 %fusion.32 = (f32[2,4,1024]{2,1,0:T(4,128)S(1)}, f32[2,4,1024,1024]{2,3,1,0:T(8,128)}) fusion(pred[1024,1024]{0,1:T(8,128)(4,1)S(1)} %iota_compare_fusion, bf16[1024,2,128,1]{0,2,3,1:T(8,128)(2,1)} %bitcast.121, bf16[1024,2,4,128]{0,3,2,1:T(8,128)(2,1)S(1)} %bitcast.117), kind=kOutput, calls=%fused_computation.96 | convolution fusion | flops 2181039104 | bytes 37257216 | tf_op jit(solution)/shard_map/sub | solution.py:40
  135.4 99.9 %collective-permute-done = bf16[1,32,128,256]{3,2,1,0:T(8,128)(2,1)} collective-permute-done((bf16[1,32,128,256]{3,2,1,0:T(8,128)(2,1)}, bf16[1,32,128,256]{3,2,1,0:T(8,128)(2,1)}, u32[]{:S(2)}, u32[]{:S(2)}) %collective-permute-start) | collective-permute-done | bytes 2097184 | tf_op jit(solution)/shard_map/ppermute | solution.py:24
  235.3 8.3 collective-permute-start.5
  248.7 125.1 %collective-permute-done.1 = bf16[1,32,128,256]{3,2,1,0:T(8,128)(2,1)} collective-permute-done((bf16[1,32,128,256]{3,2,1,0:T(8,128)(2,1)}, bf16[1,32,128,256]{3,2,1,0:T(8,128)(2,1)}, u32[]{:S(2)}, u32[]{:S(2)}) %collective-permute-start.1) | collective-permute-done | bytes 2097184 | tf_op jit(solution)/shard_map/ppermute | solution.py:24
  373.8 4.1 collective-permute-start.6
  378.0 6.3 convolution_convert_fusion.3
  390.6 28.1 %collective-permute-done.2 = bf16[1,32,128,256]{3,2,1,0:T(8,128)(2,1)} collective-permute-done((bf16[1,32,128,256]{3,2,1,0:T(8,128)(2,1)}, bf16[1,32,128,256]{3,2,1,0:T(8,128)(2,1)}, u32[]{:S(2)}, u32[]{:S(2)}) %collective-permute-start.2) | collective-permute-done | bytes 2097184 | tf_op jit(solution)/shard_map/ppermute | solution.py:24
  421.8 224.3 %collective-permute-done.3 = bf16[1,32,128,256]{3,2,1,0:T(8,128)(2,1)} collective-permute-done((bf16[1,32,128,256]{3,2,1,0:T(8,128)(2,1)}, bf16[1,32,128,256]{3,2,1,0:T(8,128)(2,1)}, u32[]{:S(2)}, u32[]{:S(2)}) %collective-permute-start.3) | collective-permute-done | bytes 2097184 | tf_op jit(solution)/shard_map/ppermute | solution.py:24
  649.2 41.0 %collective-permute-done.4 = bf16[1,32,128,256]{3,2,1,0:T(8,128)(2,1)} collective-permute-done((bf16[1,32,128,256]{3,2,1,0:T(8,128)(2,1)}, bf16[1,32,128,256]{3,2,1,0:T(8,128)(2,1)}, u32[]{:S(2)}, u32[]{:S(2)}) %collective-permute-start.4) | collective-permute-done | bytes 2097184 | tf_op jit(solution)/shard_map/ppermute | solution.py:24
  698.1 12.3 %gather_fusion.1 = bf16[128,128,256]{2,1,0:T(8,128)(2,1)} fusion(bf16[256,128,256]{2,1,0:T(8,128)(2,1)} %bitcast.114, s32[1024]{0:T(1024)S(1)} %pad_clamp_fusion), kind=kCustom, calls=%fused_computation.1 | custom fusion | bytes 16777728 | tf_op jit(solution)/shard_map/gather | solution.py:103
  710.4 12.5 %reshape.370 = bf16[8,2048,2,128]{3,2,1,0:T(2,128)(2,1)} reshape(bf16[128,128,256]{2,1,0:T(8,128)(2,1)} %gather_fusion.1) | data formatting | bytes 16777216 | tf_op jit(solution)/shard_map/reshape | solution.py:105
  723.0 12.5 %gather_fusion.3 = bf16[128,128,256]{2,1,0:T(8,128)(2,1)} fusion(bf16[256,128,256]{2,1,0:T(8,128)(2,1)} %bitcast.20, s32[1024]{0:T(1024)S(1)} %pad_clamp_fusion), kind=kCustom, calls=%fused_computation.3 | custom fusion | bytes 16777728 | tf_op jit(solution)/shard_map/gather | solution.py:102
  735.5 12.5 %reshape.371 = bf16[8,2048,2,128]{3,2,1,0:T(2,128)(2,1)} reshape(bf16[128,128,256]{2,1,0:T(8,128)(2,1)} %gather_fusion.3) | data formatting | bytes 16777216 | tf_op jit(solution)/shard_map/reshape | solution.py:104
  748.0 246.8 %while.10 = (s32[]{:T(128)}, f32[8,128,2,4,128]{1,0,4,3,2:T(8,128)}, bf16[8,2048,2,128]{3,2,1,0:T(2,128)(2,1)}, pred[8,2048]{1,0:T(8,128)(4,1)S(1)}, bf16[8,2048...) while((s32[]{:T(128)}, f32[8,128,2,4,128]{1,0,4,3,2:T(8,128)}, ...), condition=%wide.region_7.8_spmd, body=%wide.region_4.7_spmd.sunk | while | flops 1090521088 | bytes 43792992 | solution.py:117
  752.9 5.9 fusion.54
  759.6 4.1 fusion.55
  763.7 15.1 %dynamic_update_slice.45 = f32[8,128,2,4,128]{1,0,4,3,2:T(8,128)} dynamic-update-slice(f32[8,128,2,4,128]{1,0,4,3,2:T(8,128)} %get-tuple-element.144, f32[1,128,2,4,128]{1,0,4,3,2:T(1,128)S(1)} %bitcast.115, s32[]{:T(128)} %get-tuple-element.143, s32[]{:T(128)} %constant.48.clone.1..sunk, s32[]{:T(128)} %constant.48.clone.1..sunk, s32[]{:T(128)} %constant.48.clone.1..sunk, s32[]{:T(128)} %constant.48.clone.1..sunk) | dynamic-update-slice | bytes 1048580 | tf_op jit(solution)/shard_map/while/body/jit(dynamic_update_index_in_dim)/dynamic_update_slice | solution.py:117
  783.8 5.9 fusion.54
  790.5 4.1 fusion.55
  794.6 15.1 %dynamic_update_slice.45 = f32[8,128,2,4,128]{1,0,4,3,2:T(8,128)} dynamic-update-slice(f32[8,128,2,4,128]{1,0,4,3,2:T(8,128)} %get-tuple-element.144, f32[1,128,2,4,128]{1,0,4,3,2:T(1,128)S(1)} %bitcast.115, s32[]{:T(128)} %get-tuple-element.143, s32[]{:T(128)} %constant.48.clone.1..sunk, s32[]{:T(128)} %constant.48.clone.1..sunk, s32[]{:T(128)} %constant.48.clone.1..sunk, s32[]{:T(128)} %constant.48.clone.1..sunk) | dynamic-update-slice | bytes 1048580 | tf_op jit(solution)/shard_map/while/body/jit(dynamic_update_index_in_dim)/dynamic_update_slice | solution.py:117
  814.6 5.9 fusion.54
  821.3 4.1 fusion.55
  825.4 15.1 %dynamic_update_slice.45 = f32[8,128,2,4,128]{1,0,4,3,2:T(8,128)} dynamic-update-slice(f32[8,128,2,4,128]{1,0,4,3,2:T(8,128)} %get-tuple-element.144, f32[1,128,2,4,128]{1,0,4,3,2:T(1,128)S(1)} %bitcast.115, s32[]{:T(128)} %get-tuple-element.143, s32[]{:T(128)} %constant.48.clone.1..sunk, s32[]{:T(128)} %constant.48.clone.1..sunk, s32[]{:T(128)} %constant.48.clone.1..sunk, s32[]{:T(128)} %constant.48.clone.1..sunk) | dynamic-update-slice | bytes 1048580 | tf_op jit(solution)/shard_map/while/body/jit(dynamic_update_index_in_dim)/dynamic_update_slice | solution.py:117
  845.5 5.9 fusion.54
  852.2 4.1 fusion.55
  856.3 15.1 %dynamic_update_slice.45 = f32[8,128,2,4,128]{1,0,4,3,2:T(8,128)} dynamic-update-slice(f32[8,128,2,4,128]{1,0,4,3,2:T(8,128)} %get-tuple-element.144, f32[1,128,2,4,128]{1,0,4,3,2:T(1,128)S(1)} %bitcast.115, s32[]{:T(128)} %get-tuple-element.143, s32[]{:T(128)} %constant.48.clone.1..sunk, s32[]{:T(128)} %constant.48.clone.1..sunk, s32[]{:T(128)} %constant.48.clone.1..sunk, s32[]{:T(128)} %constant.48.clone.1..sunk) | dynamic-update-slice | bytes 1048580 | tf_op jit(solution)/shard_map/while/body/jit(dynamic_update_index_in_dim)/dynamic_update_slice | solution.py:117
  876.3 5.9 fusion.54
  883.0 4.1 fusion.55
  887.1 15.1 %dynamic_update_slice.45 = f32[8,128,2,4,128]{1,0,4,3,2:T(8,128)} dynamic-update-slice(f32[8,128,2,4,128]{1,0,4,3,2:T(8,128)} %get-tuple-element.144, f32[1,128,2,4,128]{1,0,4,3,2:T(1,128)S(1)} %bitcast.115, s32[]{:T(128)} %get-tuple-element.143, s32[]{:T(128)} %constant.48.clone.1..sunk, s32[]{:T(128)} %constant.48.clone.1..sunk, s32[]{:T(128)} %constant.48.clone.1..sunk, s32[]{:T(128)} %constant.48.clone.1..sunk) | dynamic-update-slice | bytes 1048580 | tf_op jit(solution)/shard_map/while/body/jit(dynamic_update_index_in_dim)/dynamic_update_slice | solution.py:117
  907.2 5.9 fusion.54
  913.8 4.1 fusion.55
  918.0 15.1 %dynamic_update_slice.45 = f32[8,128,2,4,128]{1,0,4,3,2:T(8,128)} dynamic-update-slice(f32[8,128,2,4,128]{1,0,4,3,2:T(8,128)} %get-tuple-element.144, f32[1,128,2,4,128]{1,0,4,3,2:T(1,128)S(1)} %bitcast.115, s32[]{:T(128)} %get-tuple-element.143, s32[]{:T(128)} %constant.48.clone.1..sunk, s32[]{:T(128)} %constant.48.clone.1..sunk, s32[]{:T(128)} %constant.48.clone.1..sunk, s32[]{:T(128)} %constant.48.clone.1..sunk) | dynamic-update-slice | bytes 1048580 | tf_op jit(solution)/shard_map/while/body/jit(dynamic_update_index_in_dim)/dynamic_update_slice | solution.py:117
  938.0 5.9 fusion.54
  948.8 15.1 %dynamic_update_slice.45 = f32[8,128,2,4,128]{1,0,4,3,2:T(8,128)} dynamic-update-slice(f32[8,128,2,4,128]{1,0,4,3,2:T(8,128)} %get-tuple-element.144, f32[1,128,2,4,128]{1,0,4,3,2:T(1,128)S(1)} %bitcast.115, s32[]{:T(128)} %get-tuple-element.143, s32[]{:T(128)} %constant.48.clone.1..sunk, s32[]{:T(128)} %constant.48.clone.1..sunk, s32[]{:T(128)} %constant.48.clone.1..sunk, s32[]{:T(128)} %constant.48.clone.1..sunk) | dynamic-update-slice | bytes 1048580 | tf_op jit(solution)/shard_map/while/body/jit(dynamic_update_index_in_dim)/dynamic_update_slice | solution.py:117
  968.9 5.9 fusion.54
  979.6 15.1 %dynamic_update_slice.45 = f32[8,128,2,4,128]{1,0,4,3,2:T(8,128)} dynamic-update-slice(f32[8,128,2,4,128]{1,0,4,3,2:T(8,128)} %get-tuple-element.144, f32[1,128,2,4,128]{1,0,4,3,2:T(1,128)S(1)} %bitcast.115, s32[]{:T(128)} %get-tuple-element.143, s32[]{:T(128)} %constant.48.clone.1..sunk, s32[]{:T(128)} %constant.48.clone.1..sunk, s32[]{:T(128)} %constant.48.clone.1..sunk, s32[]{:T(128)} %constant.48.clone.1..sunk) | dynamic-update-slice | bytes 1048580 | tf_op jit(solution)/shard_map/while/body/jit(dynamic_update_index_in_dim)/dynamic_update_slice | solution.py:117
  994.8 4.9 reshape.327
  999.7 13.3 %fusion.22 = bf16[1024,2,4,128]{0,3,2,1:T(8,128)(2,1)S(1)} fusion(f32[1024,2,4,128]{0,3,2,1:T(8,128)} %reshape.327, bf16[1024,2,128,1]{0,2,3,1:T(8,128)(2,1)S(1)} %bitcast.120, f32[2,4,1024,1024]{2,3,1,0:T(8,128)} %get-tuple-element.89, f32[2,4,1024]{2,1,0:T(4,128)S(1)} %get-tuple-element.88, f32[2,4]{1,0:T(2,128)S(1)} %copy-done.8, f32[2,4]{1,0:T(2,128)S(1)} %copy-done.7), kind=kOutput, calls=%fused_computation.37 | convolution fusion | flops 2168455168 | bytes 40403008 | tf_op jit(solution)/shard_map/kgqs,skd->qkgd/dot_general | solution.py:42
  1013.0 14.9 %convolution_convert_fusion = bf16[1024,4096]{1,0:T(8,128)(2,1)} fusion(bf16[1024,1024]{0,1:T(8,128)(2,1)S(1)} %bitcast.119, bf16[1024,4096]{1,0:T(8,128)(2,1)} %param.16), kind=kOutput, calls=%fused_computation.35 | convolution fusion | flops 8594128896 | bytes 18874368 | tf_op jit(solution)/shard_map/dot_general | solution.py:128
  1028.0 151.6 %reduce-scatter.2.cloned.1.call-done = bf16[1024,1024]{1,0:T(8,128)(2,1)} async-done(((bf16[1024,4096]{1,0:T(8,128)(2,1)}), bf16[1024,1024]{1,0:T(8,128)(2,1)}) %reduce-scatter.2.cloned.1.call-update) | async-done | bytes 2097168 | tf_op jit(solution)/shard_map/reduce_scatter | solution.py:129
  (98 shorter events, 93.0 us)
Async XLA Ops:
  6.5 88.9 %copy-start = (bf16[4096,256]{1,0:T(8,128)(2,1)S(1)}, bf16[4096,256]{1,0:T(8,128)(2,1)}, u32[]{:S(2)}) copy-start(bf16[4096,256]{1,0:T(8,128)(2,1)} %param.14) | copy-start | bytes 6291460
  51.4 671.6 %all-to-all-start = ((bf16[8,32,128,256]{3,2,1,0:T(8,128)(2,1)}), bf16[8,32,128,256]{3,2,1,0:T(8,128)(2,1)}, u32[]{:S(2)}, u32[]{:S(2)}) async-start(bf16[8,32,128,256]{3,2,1,0:T(8,128)(2,1)} %bitcast.110), calls=%async_computation | async-start | bytes 33554432 | tf_op jit(solution)/shard_map/all_to_all | solution.py:86
  57.1 1122.4 %reduce-scatter.2.cloned.1.call-start = ((), (), s32[]{:S(2)}) async-start(), calls=%async_computation.2 | async-start | bytes 10485760 | tf_op jit(solution)/shard_map/reduce_scatter | solution.py:129
  68.9 11.5 copy-start.2
  80.4 13.7 %copy-start.4 = (s32[8,16]{1,0:T(8,128)S(1)}, s32[8,16]{1,0:T(8,128)}, u32[]{:S(2)}) copy-start(s32[8,16]{1,0:T(8,128)} %param.20) | copy-start | bytes 1540
  80.4 13.9 %copy-start.9 = (f32[8]{0:T(128)S(1)}, f32[8]{0:T(128)}, u32[]{:S(2)}) copy-start(f32[8]{0:T(128)} %param.17) | copy-start | bytes 100
  86.4 148.9 %collective-permute-start = (bf16[1,32,128,256]{3,2,1,0:T(8,128)(2,1)}, bf16[1,32,128,256]{3,2,1,0:T(8,128)(2,1)}, u32[]{:S(2)}, u32[]{:S(2)}) collective-permute-start(bf16[1,32,128,256]{3,2,1,0:T(8,128)(2,1)} %get-tuple-element.86), channel_id=1, source_target_pairs={{0,4},{4,0},{8,12},{12,8},{16,20},{20,16},{24,28},{28,24},{1,5},{5... | collective-permute-start | bytes 6291464 | tf_op jit(solution)/shard_map/ppermute | solution.py:24
  88.3 285.5 %collective-permute-start.1 = (bf16[1,32,128,256]{3,2,1,0:T(8,128)(2,1)}, bf16[1,32,128,256]{3,2,1,0:T(8,128)(2,1)}, u32[]{:S(2)}, u32[]{:S(2)}) collective-permute-start(bf16[1,32,128,256]{3,2,1,0:T(8,128)(2,1)} %get-tuple-element.85), channel_id=1, source_target_pairs={{0,8},{4,12},{8,0},{12,4},{16,24},{20,28},{24,16},{28,20},{1,9},{5... | collective-permute-start | bytes 6291464 | tf_op jit(solution)/shard_map/ppermute | solution.py:24
  89.8 328.9 %collective-permute-start.2 = (bf16[1,32,128,256]{3,2,1,0:T(8,128)(2,1)}, bf16[1,32,128,256]{3,2,1,0:T(8,128)(2,1)}, u32[]{:S(2)}, u32[]{:S(2)}) collective-permute-start(bf16[1,32,128,256]{3,2,1,0:T(8,128)(2,1)} %get-tuple-element.84), channel_id=1, source_target_pairs={{0,12},{4,8},{8,4},{12,0},{16,28},{20,24},{24,20},{28,16},{1,13},{... | collective-permute-start | bytes 6291464 | tf_op jit(solution)/shard_map/ppermute | solution.py:24
  89.9 556.2 %collective-permute-start.3 = (bf16[1,32,128,256]{3,2,1,0:T(8,128)(2,1)}, bf16[1,32,128,256]{3,2,1,0:T(8,128)(2,1)}, u32[]{:S(2)}, u32[]{:S(2)}) collective-permute-start(bf16[1,32,128,256]{3,2,1,0:T(8,128)(2,1)} %get-tuple-element.83), channel_id=1, source_target_pairs={{0,16},{4,20},{8,24},{12,28},{16,0},{20,4},{24,8},{28,12},{1,17},{... | collective-permute-start | bytes 6291464 | tf_op jit(solution)/shard_map/ppermute | solution.py:24
  92.7 597.6 %collective-permute-start.4 = (bf16[1,32,128,256]{3,2,1,0:T(8,128)(2,1)}, bf16[1,32,128,256]{3,2,1,0:T(8,128)(2,1)}, u32[]{:S(2)}, u32[]{:S(2)}) collective-permute-start(bf16[1,32,128,256]{3,2,1,0:T(8,128)(2,1)} %get-tuple-element.82), channel_id=1, source_target_pairs={{0,20},{4,16},{8,28},{12,24},{16,4},{20,0},{24,12},{28,8},{1,21},{... | collective-permute-start | bytes 6291464 | tf_op jit(solution)/shard_map/ppermute | solution.py:24
  94.4 7.7 copy-start.6
  115.8 19.4 %copy-start.3 = (bf16[1024,1024]{0,1:T(8,128)(2,1)}, bf16[1024,1024]{0,1:T(8,128)(2,1)S(1)}, u32[]{:S(2)}) copy-start(bf16[1024,1024]{0,1:T(8,128)(2,1)S(1)} %convolution_convert_fusion.1) | copy-start | bytes 6291460
  115.8 19.4 %copy-start.5 = (s32[512]{0:T(512)S(1)}, s32[512]{0:T(512)}, u32[]{:S(2)}) copy-start(s32[512]{0:T(512)} %param.21) | copy-start | bytes 6148
  235.3 458.1 %collective-permute-start.5 = (bf16[1,32,128,256]{3,2,1,0:T(8,128)(2,1)}, bf16[1,32,128,256]{3,2,1,0:T(8,128)(2,1)}, u32[]{:S(2)}, u32[]{:S(2)}) collective-permute-start(bf16[1,32,128,256]{3,2,1,0:T(8,128)(2,1)} %get-tuple-element.81), channel_id=1, source_target_pairs={{0,24},{4,28},{8,16},{12,20},{16,8},{20,12},{24,0},{28,4},{1,25},{... | collective-permute-start | bytes 6291464 | tf_op jit(solution)/shard_map/ppermute | solution.py:24
  373.8 322.9 %collective-permute-start.6 = (bf16[1,32,128,256]{3,2,1,0:T(8,128)(2,1)}, bf16[1,32,128,256]{3,2,1,0:T(8,128)(2,1)S(1)}, u32[]{:S(2)}, u32[]{:S(2)}) collective-permute-start(bf16[1,32,128,256]{3,2,1,0:T(8,128)(2,1)} %get-tuple-element.80), channel_id=1, source_target_pairs={{0,28},{4,24},{8,20},{12,16},{16,12},{20,8},{24,4},{28,0},{1,29},{... | collective-permute-start | bytes 6291464 | tf_op jit(solution)/shard_map/ppermute | solution.py:24
  994.8 4.9 copy-start.7
  994.8 4.9 copy-start.8
  1013.0 166.6 %copy-start.1 = (bf16[4096,256]{1,0:T(8,128)(2,1)S(1)}, bf16[4096,256]{1,0:T(8,128)(2,1)}, u32[]{:S(2)}) copy-start(bf16[4096,256]{1,0:T(8,128)(2,1)} %param.14) | copy-start | bytes 6291460
Sparse Core Ops, SparseCore 0:
  1028.1 151.3 reduce-scatter.1
